TPU v7x, 32 devices: a whole 2x2x4 slice. The times are simulated.
32 devices in a mesh: tm: 4 (over x, core), particle: 2 (over y), cell: 4 (over z).
Axes of the slice: x: 2, y: 2, z: 4, core: 2. Of those that a mesh axis runs over, the one named last changes fastest.
Arguments:
- particles: float32 [4, 30, 2048], P('tm', None, 'particle'), may hold values from -50 to 50
- cell_points: float32 [4, 30, 4096], P('tm', None, 'cell'), may hold values from -50 to 50
- cell_counts: int32 [4], replicated, may hold values from 682 to 4096, as said below
- brownian: float32 [4, 30, 2048], P('tm', None, ('particle', 'cell')), may hold values from -6 to 6
Outputs:
- descent_direction: float32 [4, 30, 2048], P('tm', None, ('particle', 'cell'))
- updated_particles: float32 [4, 30, 2048], P('tm', None, ('particle', 'cell'))
Inputs may be any that keep to these rules, and one draw needn't show every extreme that they name: `cell_counts`: some time has all 4096 cells observed.
All inputs are finite; a program needn't handle non-finite values.
Results may differ from a plain program's by a relative error of at most 0.0003.
Values sent between devices are 32-bit elements; how exact they have to be, the bound alone decides.
No kernel may reach another device: no remote copies, remote signals or barrier semaphores. Data moves between devices by JAX's collectives and lax.ppermute only.
A program may use at most 64 MiB of HBM per device.

v0:
```python
import functools
import itertools
import math

import jax
import jax.numpy as jnp
from jax import lax
from jax.experimental import pallas as pl
from jax.experimental.pallas import tpu as pltpu
from jax.sharding import PartitionSpec as P


DATA_VAR = 2.0
BRIDGE_VAR = 1.5
LANGEVIN_STRIDE = 0.05
NOISE_LEVEL = 1.0
LOWEST = -1e30
LANES = 128
GROUP = 32
FIT_SCALE = math.log2(math.e) / DATA_VAR
BRIDGE_SCALE = math.log2(math.e) / BRIDGE_VAR
f32, bf16 = jnp.float32, jnp.bfloat16


def load_columns(ref, features, first, count):
    blocks = ref.shape[0] // features
    return jnp.concatenate(
        [ref[pl.ds(first + k, features, stride=blocks), :] for k in range(count)], 1
    )


def three_parts(x):
    high = x.astype(bf16).astype(f32)
    rest = x - high
    middle = rest.astype(bf16).astype(f32)
    return high, middle, rest - middle


def grouped(x, first, second):
    return jnp.concatenate([x, first, second], 0)


def target_operand(x, scale, usable=None):
    width = x.shape[1]
    zero, one = jnp.zeros((1, width), f32), jnp.ones((1, width), f32)
    norm_high, norm_middle, norm_low = three_parts(-0.5 * scale * jnp.sum(x * x, 0, keepdims=True))
    if usable is not None:
        norm_high = jnp.where(usable, norm_high, LOWEST)
        norm_middle = jnp.where(usable, norm_middle, 0.0)
        norm_low = jnp.where(usable, norm_low, 0.0)
    high, middle, low = three_parts(x)
    return jnp.concatenate(
        [
            grouped(high, norm_high, norm_middle),
            grouped(middle, norm_low, zero),
            grouped(high, one, zero),
            grouped(low, zero, zero),
            grouped(middle, zero, zero),
            grouped(high, zero, zero),
        ],
        0,
    ).astype(bf16)


def query_operand(x, scale):
    width = x.shape[1]
    zero, one = jnp.zeros((1, width), f32), jnp.ones((1, width), f32)
    high, middle, low = three_parts(x * scale)
    return (
        jnp.concatenate(
            [
                grouped(high, one, one),
                grouped(high, one, zero),
                grouped(middle, zero, zero),
                grouped(high, zero, zero),
                grouped(middle, zero, zero),
                grouped(low, zero, zero),
            ],
            0,
        )
        .astype(bf16)
        .T
    )


def weigh(scores):
    highest = jnp.max(scores, 1, keepdims=True)
    weights = jnp.exp2(scores - highest)
    weights_high = weights.astype(bf16)
    weights_low = (weights - weights_high.astype(f32)).astype(bf16)
    return highest, weights_high, weights_low


def total(highest, weights_high, weights_low, targets):
    values = targets[2 * GROUP : 5 * GROUP]
    along = (((1,), (1,)), ((), ()))
    sums = lax.dot_general(weights_high, values, along, preferred_element_type=f32)
    sums = sums + lax.dot_general(weights_low, values, along, preferred_element_type=f32)
    column = lax.broadcasted_iota(jnp.int32, sums.shape, 1)
    turned = jnp.where(column == GROUP - 1, highest, sums).T
    return turned[:GROUP] + turned[GROUP : 2 * GROUP] + turned[2 * GROUP : 3 * GROUP]


def many_sums(jobs, block=128, ahead=3):
    units = []
    for n, (queries, targets) in enumerate(jobs):
        for first in range(0, queries.shape[0], block):
            units.append((n, queries[first : first + block], targets))

    def score(unit):
        return jnp.dot(unit[1], unit[2], preferred_element_type=f32)

    found = [[] for _ in jobs]
    scored = [score(unit) for unit in units[:ahead]]
    for k, unit in enumerate(units):
        if k + ahead < len(units):
            scored.append(score(units[k + ahead]))
        found[unit[0]].append(total(*weigh(scored[k]), unit[2]))
    return [jnp.concatenate(parts, 1) for parts in found]


def merged(parts):
    if len(parts) == 1:
        return parts[0]
    highest = functools.reduce(jnp.maximum, [part[GROUP - 1 :] for part in parts])
    total = sum(part * jnp.exp2(part[GROUP - 1 :] - highest) for part in parts)
    row = lax.broadcasted_iota(jnp.int32, total.shape, 0)
    return jnp.where(row == GROUP - 1, highest, total)


def mean_of(part):
    return part / part[GROUP - 2 : GROUP - 1]


def usable_cells(count, positions_ref, which):
    return positions_ref[0:1, :] + which * positions_ref.shape[1] < count


def own_cell():
    return lax.axis_index("cell")


def share_columns(ref, features, which, share):
    blocks = share // LANES
    return load_columns(ref, features, which * blocks, blocks)


def whole(ref, features):
    return load_columns(ref, features, 0, ref.shape[0] // features)


def number_cells(positions_ref):
    positions_ref[...] = lax.broadcasted_iota(jnp.int32, positions_ref.shape, 1)


def has_far_side():
    time = lax.axis_index("tm")
    other = time - 1 + 2 * lax.rem(time, 2)
    return jnp.logical_and(other >= 0, other < lax.axis_size("tm"))


def lower_half():
    return own_cell() < lax.axis_size("cell") // 2


def either(condition, if_true, if_false):
    pl.when(condition)(if_true)
    pl.when(jnp.logical_not(condition))(if_false)


def fit_queries_of(features, share, block_ref, shares):
    columns = [
        share_columns(block_ref, features, lax.bitwise_xor(own_cell(), 2 * j), share)
        for j in shares
    ]
    return query_operand(jnp.concatenate(columns, 1), FIT_SCALE)


def fit_first(features, share, counts_ref, positions_ref, block_ref, cells_ref, *refs):
    parts_ref, queries_ref, operand_ref, count_ref = refs
    shares = parts_ref.shape[0]

    def for_shares(first):
        queries = fit_queries_of(features, share, block_ref, range(first, shares))
        queries_ref[first * share :, :] = queries
        counts = counts_ref[...].astype(f32).reshape(1, -1)
        here = lax.broadcasted_iota(jnp.int32, counts.shape, 1) == lax.axis_index("tm")
        count = jnp.sum(jnp.where(here, counts, 0.0), 1, keepdims=True).astype(jnp.int32)
        count_ref[...] = jnp.broadcast_to(count, count_ref.shape)
        usable = usable_cells(count, positions_ref, own_cell())
        targets = target_operand(whole(cells_ref, features), FIT_SCALE, usable)
        operand_ref[...] = targets
        block, ahead = (256, 1) if first == 0 else (128, 0)
        parts = many_sums([(queries, targets)], block, ahead)[0]
        for j in range(first, shares):
            at = (j - first) * share
            parts_ref[j] = parts[:, at : at + share]

    def rest():
        parts_ref[0] = jnp.zeros_like(parts_ref[0])
        queries_ref[:share, :] = jnp.zeros((share, queries_ref.shape[1]), bf16)
        for_shares(1)

    either(lower_half(), lambda: for_shares(0), rest)


def fit_early():
    return jnp.logical_and(lower_half(), has_far_side())


def fit_second(features, share, count_ref, positions_ref, queries_ref, parts_ref, *refs):
    cells_ref, operand_ref, own_fit_ref, *fit_refs = refs

    def for_shares(first):
        usable = usable_cells(count_ref[0:1, 0:1], positions_ref, lax.bitwise_xor(own_cell(), 1))
        targets = target_operand(whole(cells_ref, features), FIT_SCALE, usable)
        operand_ref[...] = targets
        block, ahead = (256, 1) if first == 0 else (128, 0)
        parts = many_sums([(queries_ref[first * share :, :], targets)], block, ahead)[0]
        for j, fit_ref in enumerate([own_fit_ref, *fit_refs]):
            if j >= first:
                at = (j - first) * share
                fit_ref[...] = merged([parts_ref[j], parts[:, at : at + share]])

    def rest():
        own_fit_ref[...] = parts_ref[0]
        for_shares(1)

    either(fit_early(), lambda: for_shares(0), rest)


def bridge_queries_of(features, share, block_ref):
    return query_operand(share_columns(block_ref, features, own_cell(), share), BRIDGE_SCALE)


def side_operand(key_ref, features):
    return target_operand(whole(key_ref, features), BRIDGE_SCALE)


def own_near(features, share, block_ref, early_ref, fit_queries_ref, *refs):
    own_ref, near_ref, *key_refs, fit_ref, pull_ref, queries_ref = refs
    queries_ref[...] = bridge_queries_of(features, share, block_ref)

    def pulls(keys, fits):
        queries = queries_ref[...]
        jobs = [(queries, side_operand(key, features)) for key in keys]
        sums = many_sums(fits + jobs)
        return sums[: len(fits)], sums[len(fits) :]

    def early():
        fit_ref[...] = early_ref[...]
        pull_ref[...] = merged(pulls(key_refs, [])[1])

    def early_end():
        fits, sums = pulls(key_refs, [(fit_queries_ref[:share, :], near_ref[...])])
        fit_ref[...] = merged([early_ref[...]] + fits)
        pull_ref[...] = merged(sums)

    def late():
        queries = fit_queries_of(features, share, block_ref, [0])
        fits, sums = pulls(key_refs, [(queries, own_ref[...]), (queries, near_ref[...])])
        fit_ref[...] = merged(fits)
        pull_ref[...] = merged(sums)

    pl.when(fit_early())(early)
    pl.when(jnp.logical_and(lower_half(), jnp.logical_not(has_far_side())))(early_end)
    pl.when(jnp.logical_not(lower_half()))(late)


def bridge(queries, key_refs, features):
    targets = [side_operand(key_ref, features) for key_ref in key_refs]
    return merged(many_sums([(queries, target) for target in targets]))


def own_far(features, queries_ref, *refs):
    *key_refs, pull_ref = refs

    @pl.when(has_far_side())
    def _():
        pull_ref[...] = bridge(queries_ref[...], key_refs, features)

    @pl.when(jnp.logical_not(has_far_side()))
    def _():
        pull_ref[...] = jnp.ones_like(pull_ref)


def finish(features, share, block_ref, noise_ref, near_ref, far_ref, *refs):
    fit_refs = refs[:-5]
    drift_out, moved_out, drift_ref, moved_ref, sem = refs[-5:]
    per_share = share // LANES
    first = own_cell() * per_share
    time, times = lax.axis_index("tm"), lax.axis_size("tm")
    step = 1 - 2 * lax.rem(time, 2)
    fit_mean = mean_of(merged([ref[...] for ref in fit_refs]))
    sides = [
        (mean_of(ref[...]), jnp.logical_and(other >= 0, other < times))
        for ref, other in ((near_ref, time + step), (far_ref, time - step))
    ]
    for k in range(per_share):
        lanes = slice(k * LANES, (k + 1) * LANES)
        x = block_ref[pl.ds(first + k, features, stride=block_ref.shape[0] // features), :]
        gradient = (x - fit_mean[:features, lanes]) / DATA_VAR
        for mean, present in sides:
            gradient = gradient + jnp.where(present, (x - mean[:features, lanes]) / BRIDGE_VAR, 0.0)
        drift = -gradient
        drift_ref[:, 0, lanes] = drift
        moved_ref[:, 0, lanes] = (
            x
            + LANGEVIN_STRIDE * drift
            + math.sqrt(2.0 * LANGEVIN_STRIDE * NOISE_LEVEL) * noise_ref[:, 0, lanes]
        )
    copies = [
        pltpu.make_async_copy(drift_ref, drift_out, sem.at[0]),
        pltpu.make_async_copy(moved_ref, moved_out, sem.at[1]),
    ]
    for copy in copies:
        copy.start()
    for copy in copies:
        copy.wait()


VMEM = pl.BlockSpec(memory_space=pltpu.VMEM)


def call(kernel, out_shape, args, flops, out_spec=VMEM, scratch=()):
    return pl.pallas_call(
        kernel,
        out_shape=out_shape,
        in_specs=[VMEM] * len(args),
        out_specs=jax.tree.map(lambda _: out_spec, out_shape),
        scratch_shapes=scratch,
        compiler_params=pltpu.CompilerParams(vmem_limit_bytes=24 * 1024 * 1024),
        cost_estimate=pl.CostEstimate(
            flops=flops, bytes_accessed=4 * sum(a.size for a in args), transcendentals=0
        ),
    )(*args)


def near_pair(t):
    return t + 1 - 2 * (t % 2)


def far_pair(t):
    return t - 1 + 2 * (t % 2)


def shards(particles, cell_points, cell_counts, brownian):
    features = particles.shape[1]
    block = particles.reshape(-1, LANES)
    cells = cell_points.reshape(-1, LANES)
    noise = brownian.transpose(1, 0, 2)
    share = brownian.shape[2]
    cell_size, times, blocks = (lax.axis_size(name) for name in ("cell", "tm", "particle"))
    shares = cell_size // 2
    width = cell_points.shape[2]

    def over_cell(x, by):
        return lax.ppermute(x, "cell", [(c, c ^ by) for c in range(cell_size)])

    def over_time(pair, by):
        pairs = []
        for t, p, c in itertools.product(range(times), range(blocks), range(cell_size)):
            other, q, d = pair(t), (p + by) % blocks, c
            if not 0 <= other < times:
                other, q, d = (t, p, c ^ 1) if by == 0 else (t, q, c)
            pairs.append(((t * blocks + p) * cell_size + c, (other * blocks + q) * cell_size + d))
        return lax.ppermute(block, ("tm", "particle", "cell"), pairs)

    near_cells = over_cell(cells, 1)
    keys = {}
    for side, pair in (("near", near_pair), ("far", far_pair)):
        keys[side] = [over_time(pair, 0)]
        keys[side] += [over_time(pair, by) for by in range(1, blocks)]

    part = jax.ShapeDtypeStruct((GROUP, share), f32)
    operand = jax.ShapeDtypeStruct((6 * GROUP, width), bf16)
    own_queries = jax.ShapeDtypeStruct((share, 6 * GROUP), bf16)
    positions = call(number_cells, jax.ShapeDtypeStruct((8, width), jnp.int32), (), 10**10)
    parts, fit_queries, own_operand, count = call(
        functools.partial(fit_first, features, share),
        (
            jax.ShapeDtypeStruct((shares, GROUP, share), f32),
            jax.ShapeDtypeStruct((shares * share, 6 * GROUP), bf16),
            operand,
            jax.ShapeDtypeStruct((8, LANES), jnp.int32),
        ),
        (cell_counts, positions, block, cells),
        10**9,
    )
    near_operand, early_fit, *sent_fits = call(
        functools.partial(fit_second, features, share),
        (operand,) + (part,) * shares,
        (count, positions, fit_queries, parts, near_cells),
        10**9,
    )
    fits = [over_cell(x, 2 * by) for by, x in zip(range(1, shares), sent_fits)]
    own_fit, near_pull, bridge_queries = call(
        functools.partial(own_near, features, share),
        (part, part, own_queries),
        (block, early_fit, fit_queries, own_operand, near_operand, *keys["near"]),
        10**9,
    )
    far_pull = call(
        functools.partial(own_far, features), part, (bridge_queries, *keys["far"]), 10**9
    )
    out = jax.ShapeDtypeStruct(noise.shape, f32)
    drift, moved = call(
        functools.partial(finish, features, share),
        (out, out),
        (block, noise, near_pull, far_pull, own_fit, *fits),
        10**6,
        out_spec=pl.BlockSpec(memory_space=pltpu.HBM),
        scratch=[
            pltpu.VMEM(noise.shape, f32),
            pltpu.VMEM(noise.shape, f32),
            pltpu.SemaphoreType.DMA((2,)),
        ],
    )
    return drift.transpose(1, 0, 2), moved.transpose(1, 0, 2)


def solution(mesh):
    in_specs = (
        P("tm", None, "particle"),
        P("tm", None, "cell"),
        P(),
        P("tm", None, ("particle", "cell")),
    )
    out_specs = (P("tm", None, ("particle", "cell")), P("tm", None, ("particle", "cell")))
    return jax.shard_map(shards, mesh=mesh, in_specs=in_specs, out_specs=out_specs, check_vma=False)
```

profile of v0, /device:TPU:0, one launch (start us, length us, event | category | flops | bytes accessed | tf_op | source)
XLA Modules:
  0.0 18.4 jit_solution(5682734655856974354)
XLA Ops:
  0.6 0.6 %collective-permute-start.1 = (f32[240,128]{1,0:T(8,128)}, f32[240,128]{1,0:T(8,128)S(1)}, u32[]{:S(2)}, u32[]{:S(2)}) collective-permute-start(f32[240,128]{1,0:T(8,128)} %bitcast.5), channel_id=1, source_target_pairs={{0,8},{1,9},{2,10},{3,11},{4,12},{5,13},{6,14},{7,15},{8,0},{9,1},... | collective-permute-start | bytes 368648 | tf_op jit(solution)/shard_map/ppermute | solution.py:367
  1.2 2.6 %collective-permute-start.2 = (f32[240,128]{1,0:T(8,128)}, f32[240,128]{1,0:T(8,128)S(1)}, u32[]{:S(2)}, u32[]{:S(2)}) collective-permute-start(f32[240,128]{1,0:T(8,128)} %bitcast.6), channel_id=1, source_target_pairs={{0,12},{1,13},{2,14},{3,15},{4,8},{5,9},{6,10},{7,11},{8,4},{9,5},... | collective-permute-start | bytes 368648 | tf_op jit(solution)/shard_map/ppermute | solution.py:367
  3.8 1.6 %collective-permute-start.3 = (f32[240,128]{1,0:T(8,128)}, f32[240,128]{1,0:T(8,128)S(1)}, u32[]{:S(2)}, u32[]{:S(2)}) collective-permute-start(f32[240,128]{1,0:T(8,128)} %bitcast.7), channel_id=1, source_target_pairs={{0,1},{1,0},{2,3},{3,2},{4,5},{5,4},{6,7},{7,6},{8,16},{9,17},{10,... | collective-permute-start | bytes 368648 | tf_op jit(solution)/shard_map/ppermute | solution.py:367
  5.4 0.5 %collective-permute-start.4 = (f32[240,128]{1,0:T(8,128)}, f32[240,128]{1,0:T(8,128)S(1)}, u32[]{:S(2)}, u32[]{:S(2)}) collective-permute-start(f32[240,128]{1,0:T(8,128)} %bitcast.8), channel_id=1, source_target_pairs={{0,4},{1,5},{2,6},{3,7},{4,0},{5,1},{6,2},{7,3},{8,20},{9,21},{10,... | collective-permute-start | bytes 368648 | tf_op jit(solution)/shard_map/ppermute | solution.py:367
  5.9 0.0 copy-start
  5.9 0.0 copy-start.2
  5.9 0.0 copy-start.3
  5.9 0.0 collective-permute-start
  5.9 0.9 %copy-done = f32[1,30,1024]{2,0,1:T(1,128)S(1)} copy-done((f32[1,30,1024]{2,0,1:T(1,128)S(1)}, f32[1,30,1024]{2,0,1:T(1,128)}, u32[]{:S(2)}) %copy-start) | copy-done | bytes 122904
  6.8 0.0 copy-done.2
  6.8 0.0 copy-done.3
  6.9 1.5 %shard_map.60 = (f32[2,32,256]{2,1,0:T(8,128)S(1)}, bf16[512,192]{1,0:T(8,128)(2,1)S(1)}, bf16[192,1024]{1,0:T(8,128)(2,1)S(1)}, s32[8,128]{1,0:T(8,128)S(1)}) custom-call(s32[4]{0:T(128)S(1)} %copy-done.3, s32[8,1024]{1,0:T(8,128)S(1)} %shard_map.59.positions_ref, f32[240,128]{1,0:T(8,128)S(1)} %bitcast.9, f32[240,128]{1,0:T(8,128)S(1)} %bitcast.14), custom_call_target="tpu_custom_call" | custom-call | flops 1000000000 | bytes 278544 | tf_op jit(solution)/shard_map/pallas_call | solution.py:326
  8.3 3.2 %collective-permute-done.refs_0_ = f32[240,128]{1,0:T(8,128)S(1)} collective-permute-done((f32[240,128]{1,0:T(8,128)}, f32[240,128]{1,0:T(8,128)S(1)}, u32[]{:S(2)}, u32[]{:S(2)}) %collective-permute-start) | collective-permute-done | bytes 122912 | tf_op jit(solution)/shard_map/ppermute | solution.py:358
  11.5 0.9 %shard_map.61 = (bf16[192,1024]{1,0:T(8,128)(2,1)S(1)}, f32[32,256]{1,0:T(8,128)S(1)}, f32[32,256]{1,0:T(8,128)S(1)}) custom-call(s32[8,128]{1,0:T(8,128)S(1)} %get-tuple-element.14.count_ref, s32[8,1024]{1,0:T(8,128)S(1)} %shard_map.59.positions_ref, bf16[512,192]{1,0:T(8,128)(2,1)S(1)} %get-tuple-element.15.queries_ref.fit_queries_ref, ...), custom_call_target="tpu_custom_call" | custom-call | flops 1000000000 | bytes 618496 | tf_op jit(solution)/shard_map/pallas_call | solution.py:326
  12.5 2.7 %collective-permute-start.5 = (f32[32,256]{1,0:T(8,128)S(1)}, f32[32,256]{1,0:T(8,128)S(1)}, u32[]{:S(2)}, u32[]{:S(2)}) collective-permute-start(f32[32,256]{1,0:T(8,128)S(1)} %get-tuple-element.23), channel_id=1, source_target_pairs={{0,2},{1,3},{2,0},{3,1},{4,6},{5,7},{6,4},{7,5},{8,10},{9,11},{10,... | collective-permute-start | bytes 98312 | tf_op jit(solution)/shard_map/ppermute | solution.py:358
  15.1 0.0 collective-permute-done.1.refs_2_
  15.1 0.0 collective-permute-done.2.refs_3_
  15.1 1.7 %shard_map.62 = (f32[32,256]{1,0:T(8,128)S(1)}, f32[32,256]{1,0:T(8,128)S(1)}, bf16[256,192]{1,0:T(8,128)(2,1)S(1)}) custom-call(f32[240,128]{1,0:T(8,128)S(1)} %bitcast.10, f32[32,256]{1,0:T(8,128)S(1)} %get-tuple-element.17.early_ref, bf16[512,192]{1,0:T(8,128)(2,1)S(1)} %get-tuple-element.15.queries_ref.fit_queries_ref, ...), custom_call_target="tpu_custom_call" | custom-call | flops 1000000000 | bytes 2367488 | tf_op jit(solution)/shard_map/pallas_call | solution.py:326
  16.8 0.0 collective-permute-done.3.refs_0_
  16.8 0.0 collective-permute-done.4.refs_1_
  16.9 0.0 copy-start.1
  16.9 0.8 %collective-permute-done.5.refs_1_ = f32[32,256]{1,0:T(8,128)S(1)} collective-permute-done((f32[32,256]{1,0:T(8,128)S(1)}, f32[32,256]{1,0:T(8,128)S(1)}, u32[]{:S(2)}, u32[]{:S(2)}) %collective-permute-start.5) | collective-permute-done | bytes 32800 | tf_op jit(solution)/shard_map/ppermute | solution.py:358
  17.7 0.0 copy-done.1
  17.7 0.7 %shard_map.64 = (f32[30,1,256]{2,1,0:T(1,128)}, f32[30,1,256]{2,1,0:T(1,128)}) custom-call(f32[240,128]{1,0:T(8,128)S(1)} %bitcast.11, f32[30,1,256]{2,1,0:T(1,128)S(1)} %bitcast.12, f32[32,256]{1,0:T(8,128)S(1)} %get-tuple-element.20.near_ref, f32[32,256]{1,0:T(8,128)S(1)} %shard_map.63.far_ref, f32[32,256]{1,0:T(8,128)S(1)} %get-tuple-element.22.refs_0_, ...), custom_call_target="tpu_custom_call" | custom-call | flops 1000000 | bytes 284672 | tf_op jit(solution)/shard_map/pallas_call | solution.py:326
  (2 shorter events, 0.0 us)
Async XLA Ops:
  0.6 14.5 %collective-permute-start.1 = (f32[240,128]{1,0:T(8,128)}, f32[240,128]{1,0:T(8,128)S(1)}, u32[]{:S(2)}, u32[]{:S(2)}) collective-permute-start(f32[240,128]{1,0:T(8,128)} %bitcast.5), channel_id=1, source_target_pairs={{0,8},{1,9},{2,10},{3,11},{4,12},{5,13},{6,14},{7,15},{8,0},{9,1},... | collective-permute-start | bytes 368648 | tf_op jit(solution)/shard_map/ppermute | solution.py:367
  1.2 14.0 %collective-permute-start.2 = (f32[240,128]{1,0:T(8,128)}, f32[240,128]{1,0:T(8,128)S(1)}, u32[]{:S(2)}, u32[]{:S(2)}) collective-permute-start(f32[240,128]{1,0:T(8,128)} %bitcast.6), channel_id=1, source_target_pairs={{0,12},{1,13},{2,14},{3,15},{4,8},{5,9},{6,10},{7,11},{8,4},{9,5},... | collective-permute-start | bytes 368648 | tf_op jit(solution)/shard_map/ppermute | solution.py:367
  3.8 13.0 %collective-permute-start.3 = (f32[240,128]{1,0:T(8,128)}, f32[240,128]{1,0:T(8,128)S(1)}, u32[]{:S(2)}, u32[]{:S(2)}) collective-permute-start(f32[240,128]{1,0:T(8,128)} %bitcast.7), channel_id=1, source_target_pairs={{0,1},{1,0},{2,3},{3,2},{4,5},{5,4},{6,7},{7,6},{8,16},{9,17},{10,... | collective-permute-start | bytes 368648 | tf_op jit(solution)/shard_map/ppermute | solution.py:367
  5.4 11.5 %collective-permute-start.4 = (f32[240,128]{1,0:T(8,128)}, f32[240,128]{1,0:T(8,128)S(1)}, u32[]{:S(2)}, u32[]{:S(2)}) collective-permute-start(f32[240,128]{1,0:T(8,128)} %bitcast.8), channel_id=1, source_target_pairs={{0,4},{1,5},{2,6},{3,7},{4,0},{5,1},{6,2},{7,3},{8,20},{9,21},{10,... | collective-permute-start | bytes 368648 | tf_op jit(solution)/shard_map/ppermute | solution.py:367
  5.9 0.9 %copy-start = (f32[1,30,1024]{2,0,1:T(1,128)S(1)}, f32[1,30,1024]{2,0,1:T(1,128)}, u32[]{:S(2)}) copy-start(f32[1,30,1024]{2,0,1:T(1,128)} %param.4) | copy-start | bytes 368644
  5.9 1.0 %copy-start.2 = (f32[1,30,1024]{2,0,1:T(1,128)S(1)}, f32[1,30,1024]{2,0,1:T(1,128)}, u32[]{:S(2)}) copy-start(f32[1,30,1024]{2,0,1:T(1,128)} %param.5) | copy-start | bytes 368644
  5.9 1.0 %copy-start.3 = (s32[4]{0:T(128)S(1)}, s32[4]{0:T(128)}, u32[]{:S(2)}) copy-start(s32[4]{0:T(128)} %counts_ref.1) | copy-start | bytes 52
  5.9 5.6 %collective-permute-start = (f32[240,128]{1,0:T(8,128)}, f32[240,128]{1,0:T(8,128)S(1)}, u32[]{:S(2)}, u32[]{:S(2)}) collective-permute-start(f32[240,128]{1,0:T(8,128)} %bitcast.13), channel_id=1, source_target_pairs={{0,1},{1,0},{2,3},{3,2},{4,5},{5,4},{6,7},{7,6},{8,9},{9,8},{10,11... | collective-permute-start | bytes 368648 | tf_op jit(solution)/shard_map/ppermute | solution.py:358
  12.5 5.2 %collective-permute-start.5 = (f32[32,256]{1,0:T(8,128)S(1)}, f32[32,256]{1,0:T(8,128)S(1)}, u32[]{:S(2)}, u32[]{:S(2)}) collective-permute-start(f32[32,256]{1,0:T(8,128)S(1)} %get-tuple-element.23), channel_id=1, source_target_pairs={{0,2},{1,3},{2,0},{3,1},{4,6},{5,7},{6,4},{7,5},{8,10},{9,11},{10,... | collective-permute-start | bytes 98312 | tf_op jit(solution)/shard_map/ppermute | solution.py:358
  16.9 0.8 %copy-start.1 = (f32[1,30,256]{2,0,1:T(1,128)S(1)}, f32[1,30,256]{2,0,1:T(1,128)}, u32[]{:S(2)}) copy-start(f32[1,30,256]{2,0,1:T(1,128)} %param.7) | copy-start | bytes 92164
where the time goes:
time: 18.6 us; the launch traced here: 18.4 us
  starting transfers between devices  7.95 us (43%)
  Pallas kernels  4.83 us (26%)
  waiting for transfers between devices  4.02 us (22%)
  local copies, waits for them, and re-layouts  0.93 us (5%)
  between operations  0.69 us (4%)
    ppermute x4, starting transfers between devices, over_time(): return lax.ppermute(block, ('tm', 'particle', 'cell'), pairs)  5.26 us
    pallas_call x6, Pallas kernels, call(): pl.pallas_call(kernel, out_shape=out_shape, in_specs=[VMEM] * len(args),...  4.83 us
    ppermute x2, waiting for transfers between devices, over_cell(): return lax.ppermute(x, 'cell', [(c, c ^ by) for c in range(cell_size)])  4.01 us
    ppermute x2, starting transfers between devices, over_cell(): return lax.ppermute(x, 'cell', [(c, c ^ by) for c in range(cell_size)])  2.69 us
    unnamed x8, local copies, waits for them, and re-layouts  0.93 us
  transfers between devices with their start and end apart: 6, of which 2 were waited for; matrix products, arithmetic and copies ran while one was open for 0% of the time, Pallas kernels for 22%

commit v1 on v0

--- a/solution.py
+++ b/solution.py
@@ -190,7 +190,7 @@
         usable = usable_cells(count, positions_ref, own_cell())
         targets = target_operand(whole(cells_ref, features), FIT_SCALE, usable)
         operand_ref[...] = targets
-        block, ahead = (256, 1) if first == 0 else (128, 0)
+        block, ahead = (128, 3) if first == 0 else (128, 0)
         parts = many_sums([(queries, targets)], block, ahead)[0]
         for j in range(first, shares):
             at = (j - first) * share
@@ -205,7 +205,8 @@
 
 
 def fit_early():
-    return jnp.logical_and(lower_half(), has_far_side())
+    odd = lax.rem(lax.axis_index("tm"), 2) == 1
+    return jnp.logical_and(odd, jnp.logical_and(lower_half(), has_far_side()))
 
 
 def fit_second(features, share, count_ref, positions_ref, queries_ref, parts_ref, *refs):
@@ -215,7 +216,7 @@
         usable = usable_cells(count_ref[0:1, 0:1], positions_ref, lax.bitwise_xor(own_cell(), 1))
         targets = target_operand(whole(cells_ref, features), FIT_SCALE, usable)
         operand_ref[...] = targets
-        block, ahead = (256, 1) if first == 0 else (128, 0)
+        block, ahead = (128, 3) if first == 0 else (128, 0)
         parts = many_sums([(queries_ref[first * share :, :], targets)], block, ahead)[0]
         for j, fit_ref in enumerate([own_fit_ref, *fit_refs]):
             if j >= first:
@@ -263,7 +264,7 @@
         pull_ref[...] = merged(sums)
 
     pl.when(fit_early())(early)
-    pl.when(jnp.logical_and(lower_half(), jnp.logical_not(has_far_side())))(early_end)
+    pl.when(jnp.logical_and(lower_half(), jnp.logical_not(fit_early())))(early_end)
     pl.when(jnp.logical_not(lower_half()))(late)
 
 

time: 18.6 us -> 18.6 us (level)
  transfers between devices with their start and end apart: 6 -> 6, of which waited for: 2 -> 2; matrix products, arithmetic and copies ran while one was open for 0% -> 0% of each run, Pallas kernels for 22% -> 21%
where the time goes in v1:
time: 18.6 us; the launch traced here: 18.4 us
  starting transfers between devices  7.95 us (43%)
  Pallas kernels  4.65 us (25%)
  waiting for transfers between devices  4.18 us (22%)
  local copies, waits for them, and re-layouts  0.93 us (5%)
  between operations  0.69 us (4%)
    ppermute x4, starting transfers between devices, over_time(): return lax.ppermute(block, ('tm', 'particle', 'cell'), pairs)  5.26 us
    pallas_call x6, Pallas kernels, call(): pl.pallas_call(kernel, out_shape=out_shape, in_specs=[VMEM] * len(args),...  4.65 us
    ppermute x2, waiting for transfers between devices, over_cell(): return lax.ppermute(x, 'cell', [(c, c ^ by) for c in range(cell_size)])  4.17 us
    ppermute x2, starting transfers between devices, over_cell(): return lax.ppermute(x, 'cell', [(c, c ^ by) for c in range(cell_size)])  2.69 us
    unnamed x8, local copies, waits for them, and re-layouts  0.93 us
  transfers between devices with their start and end apart: 6, of which 2 were waited for; matrix products, arithmetic and copies ran while one was open for 0% of the time, Pallas kernels for 21%

profile of v1, /device:TPU:0, one launch (start us, length us, event | category | flops | bytes accessed | tf_op | source)
XLA Modules:
  0.0 18.4 jit_solution(8202428036078067633)
XLA Ops:
  0.6 0.6 %collective-permute-start.1 = (f32[240,128]{1,0:T(8,128)}, f32[240,128]{1,0:T(8,128)S(1)}, u32[]{:S(2)}, u32[]{:S(2)}) collective-permute-start(f32[240,128]{1,0:T(8,128)} %bitcast.5), channel_id=1, source_target_pairs={{0,8},{1,9},{2,10},{3,11},{4,12},{5,13},{6,14},{7,15},{8,0},{9,1},... | collective-permute-start | bytes 368648 | tf_op jit(solution)/shard_map/ppermute | solution.py:368
  1.2 2.6 %collective-permute-start.2 = (f32[240,128]{1,0:T(8,128)}, f32[240,128]{1,0:T(8,128)S(1)}, u32[]{:S(2)}, u32[]{:S(2)}) collective-permute-start(f32[240,128]{1,0:T(8,128)} %bitcast.6), channel_id=1, source_target_pairs={{0,12},{1,13},{2,14},{3,15},{4,8},{5,9},{6,10},{7,11},{8,4},{9,5},... | collective-permute-start | bytes 368648 | tf_op jit(solution)/shard_map/ppermute | solution.py:368
  3.8 1.6 %collective-permute-start.3 = (f32[240,128]{1,0:T(8,128)}, f32[240,128]{1,0:T(8,128)S(1)}, u32[]{:S(2)}, u32[]{:S(2)}) collective-permute-start(f32[240,128]{1,0:T(8,128)} %bitcast.7), channel_id=1, source_target_pairs={{0,1},{1,0},{2,3},{3,2},{4,5},{5,4},{6,7},{7,6},{8,16},{9,17},{10,... | collective-permute-start | bytes 368648 | tf_op jit(solution)/shard_map/ppermute | solution.py:368
  5.4 0.5 %collective-permute-start.4 = (f32[240,128]{1,0:T(8,128)}, f32[240,128]{1,0:T(8,128)S(1)}, u32[]{:S(2)}, u32[]{:S(2)}) collective-permute-start(f32[240,128]{1,0:T(8,128)} %bitcast.8), channel_id=1, source_target_pairs={{0,4},{1,5},{2,6},{3,7},{4,0},{5,1},{6,2},{7,3},{8,20},{9,21},{10,... | collective-permute-start | bytes 368648 | tf_op jit(solution)/shard_map/ppermute | solution.py:368
  5.9 0.0 copy-start
  5.9 0.0 copy-start.2
  5.9 0.0 copy-start.3
  5.9 0.0 collective-permute-start
  5.9 0.9 %copy-done = f32[1,30,1024]{2,0,1:T(1,128)S(1)} copy-done((f32[1,30,1024]{2,0,1:T(1,128)S(1)}, f32[1,30,1024]{2,0,1:T(1,128)}, u32[]{:S(2)}) %copy-start) | copy-done | bytes 122904
  6.8 0.0 copy-done.2
  6.8 0.0 copy-done.3
  6.9 1.3 %shard_map.60 = (f32[2,32,256]{2,1,0:T(8,128)S(1)}, bf16[512,192]{1,0:T(8,128)(2,1)S(1)}, bf16[192,1024]{1,0:T(8,128)(2,1)S(1)}, s32[8,128]{1,0:T(8,128)S(1)}) custom-call(s32[4]{0:T(128)S(1)} %copy-done.3, s32[8,1024]{1,0:T(8,128)S(1)} %shard_map.59.positions_ref, f32[240,128]{1,0:T(8,128)S(1)} %bitcast.9, f32[240,128]{1,0:T(8,128)S(1)} %bitcast.14), custom_call_target="tpu_custom_call" | custom-call | flops 1000000000 | bytes 278544 | tf_op jit(solution)/shard_map/pallas_call | solution.py:327
  8.1 3.4 %collective-permute-done.refs_0_ = f32[240,128]{1,0:T(8,128)S(1)} collective-permute-done((f32[240,128]{1,0:T(8,128)}, f32[240,128]{1,0:T(8,128)S(1)}, u32[]{:S(2)}, u32[]{:S(2)}) %collective-permute-start) | collective-permute-done | bytes 122912 | tf_op jit(solution)/shard_map/ppermute | solution.py:359
  11.5 0.9 %shard_map.61 = (bf16[192,1024]{1,0:T(8,128)(2,1)S(1)}, f32[32,256]{1,0:T(8,128)S(1)}, f32[32,256]{1,0:T(8,128)S(1)}) custom-call(s32[8,128]{1,0:T(8,128)S(1)} %get-tuple-element.14.count_ref, s32[8,1024]{1,0:T(8,128)S(1)} %shard_map.59.positions_ref, bf16[512,192]{1,0:T(8,128)(2,1)S(1)} %get-tuple-element.15.queries_ref.fit_queries_ref, ...), custom_call_target="tpu_custom_call" | custom-call | flops 1000000000 | bytes 618496 | tf_op jit(solution)/shard_map/pallas_call | solution.py:327
  12.5 2.7 %collective-permute-start.5 = (f32[32,256]{1,0:T(8,128)S(1)}, f32[32,256]{1,0:T(8,128)S(1)}, u32[]{:S(2)}, u32[]{:S(2)}) collective-permute-start(f32[32,256]{1,0:T(8,128)S(1)} %get-tuple-element.23), channel_id=1, source_target_pairs={{0,2},{1,3},{2,0},{3,1},{4,6},{5,7},{6,4},{7,5},{8,10},{9,11},{10,... | collective-permute-start | bytes 98312 | tf_op jit(solution)/shard_map/ppermute | solution.py:359
  15.1 0.0 collective-permute-done.1.refs_2_
  15.1 0.0 collective-permute-done.2.refs_3_
  15.1 1.7 %shard_map.62 = (f32[32,256]{1,0:T(8,128)S(1)}, f32[32,256]{1,0:T(8,128)S(1)}, bf16[256,192]{1,0:T(8,128)(2,1)S(1)}) custom-call(f32[240,128]{1,0:T(8,128)S(1)} %bitcast.10, f32[32,256]{1,0:T(8,128)S(1)} %get-tuple-element.17.early_ref, bf16[512,192]{1,0:T(8,128)(2,1)S(1)} %get-tuple-element.15.queries_ref.fit_queries_ref, ...), custom_call_target="tpu_custom_call" | custom-call | flops 1000000000 | bytes 2367488 | tf_op jit(solution)/shard_map/pallas_call | solution.py:327
  16.8 0.0 collective-permute-done.3.refs_0_
  16.8 0.0 collective-permute-done.4.refs_1_
  16.9 0.0 copy-start.1
  16.9 0.8 %collective-permute-done.5.refs_1_ = f32[32,256]{1,0:T(8,128)S(1)} collective-permute-done((f32[32,256]{1,0:T(8,128)S(1)}, f32[32,256]{1,0:T(8,128)S(1)}, u32[]{:S(2)}, u32[]{:S(2)}) %collective-permute-start.5) | collective-permute-done | bytes 32800 | tf_op jit(solution)/shard_map/ppermute | solution.py:359
  17.7 0.0 copy-done.1
  17.7 0.7 %shard_map.64 = (f32[30,1,256]{2,1,0:T(1,128)}, f32[30,1,256]{2,1,0:T(1,128)}) custom-call(f32[240,128]{1,0:T(8,128)S(1)} %bitcast.11, f32[30,1,256]{2,1,0:T(1,128)S(1)} %bitcast.12, f32[32,256]{1,0:T(8,128)S(1)} %get-tuple-element.20.near_ref, f32[32,256]{1,0:T(8,128)S(1)} %shard_map.63.far_ref, f32[32,256]{1,0:T(8,128)S(1)} %get-tuple-element.22.refs_0_, ...), custom_call_target="tpu_custom_call" | custom-call | flops 1000000 | bytes 284672 | tf_op jit(solution)/shard_map/pallas_call | solution.py:327
  (2 shorter events, 0.0 us)
Async XLA Ops:
  0.6 14.5 %collective-permute-start.1 = (f32[240,128]{1,0:T(8,128)}, f32[240,128]{1,0:T(8,128)S(1)}, u32[]{:S(2)}, u32[]{:S(2)}) collective-permute-start(f32[240,128]{1,0:T(8,128)} %bitcast.5), channel_id=1, source_target_pairs={{0,8},{1,9},{2,10},{3,11},{4,12},{5,13},{6,14},{7,15},{8,0},{9,1},... | collective-permute-start | bytes 368648 | tf_op jit(solution)/shard_map/ppermute | solution.py:368
  1.2 14.0 %collective-permute-start.2 = (f32[240,128]{1,0:T(8,128)}, f32[240,128]{1,0:T(8,128)S(1)}, u32[]{:S(2)}, u32[]{:S(2)}) collective-permute-start(f32[240,128]{1,0:T(8,128)} %bitcast.6), channel_id=1, source_target_pairs={{0,12},{1,13},{2,14},{3,15},{4,8},{5,9},{6,10},{7,11},{8,4},{9,5},... | collective-permute-start | bytes 368648 | tf_op jit(solution)/shard_map/ppermute | solution.py:368
  3.8 13.0 %collective-permute-start.3 = (f32[240,128]{1,0:T(8,128)}, f32[240,128]{1,0:T(8,128)S(1)}, u32[]{:S(2)}, u32[]{:S(2)}) collective-permute-start(f32[240,128]{1,0:T(8,128)} %bitcast.7), channel_id=1, source_target_pairs={{0,1},{1,0},{2,3},{3,2},{4,5},{5,4},{6,7},{7,6},{8,16},{9,17},{10,... | collective-permute-start | bytes 368648 | tf_op jit(solution)/shard_map/ppermute | solution.py:368
  5.4 11.5 %collective-permute-start.4 = (f32[240,128]{1,0:T(8,128)}, f32[240,128]{1,0:T(8,128)S(1)}, u32[]{:S(2)}, u32[]{:S(2)}) collective-permute-start(f32[240,128]{1,0:T(8,128)} %bitcast.8), channel_id=1, source_target_pairs={{0,4},{1,5},{2,6},{3,7},{4,0},{5,1},{6,2},{7,3},{8,20},{9,21},{10,... | collective-permute-start | bytes 368648 | tf_op jit(solution)/shard_map/ppermute | solution.py:368
  5.9 0.9 %copy-start = (f32[1,30,1024]{2,0,1:T(1,128)S(1)}, f32[1,30,1024]{2,0,1:T(1,128)}, u32[]{:S(2)}) copy-start(f32[1,30,1024]{2,0,1:T(1,128)} %param.4) | copy-start | bytes 368644
  5.9 1.0 %copy-start.2 = (f32[1,30,1024]{2,0,1:T(1,128)S(1)}, f32[1,30,1024]{2,0,1:T(1,128)}, u32[]{:S(2)}) copy-start(f32[1,30,1024]{2,0,1:T(1,128)} %param.5) | copy-start | bytes 368644
  5.9 1.0 %copy-start.3 = (s32[4]{0:T(128)S(1)}, s32[4]{0:T(128)}, u32[]{:S(2)}) copy-start(s32[4]{0:T(128)} %counts_ref.1) | copy-start | bytes 52
  5.9 5.6 %collective-permute-start = (f32[240,128]{1,0:T(8,128)}, f32[240,128]{1,0:T(8,128)S(1)}, u32[]{:S(2)}, u32[]{:S(2)}) collective-permute-start(f32[240,128]{1,0:T(8,128)} %bitcast.13), channel_id=1, source_target_pairs={{0,1},{1,0},{2,3},{3,2},{4,5},{5,4},{6,7},{7,6},{8,9},{9,8},{10,11... | collective-permute-start | bytes 368648 | tf_op jit(solution)/shard_map/ppermute | solution.py:359
  12.5 5.2 %collective-permute-start.5 = (f32[32,256]{1,0:T(8,128)S(1)}, f32[32,256]{1,0:T(8,128)S(1)}, u32[]{:S(2)}, u32[]{:S(2)}) collective-permute-start(f32[32,256]{1,0:T(8,128)S(1)} %get-tuple-element.23), channel_id=1, source_target_pairs={{0,2},{1,3},{2,0},{3,1},{4,6},{5,7},{6,4},{7,5},{8,10},{9,11},{10,... | collective-permute-start | bytes 98312 | tf_op jit(solution)/shard_map/ppermute | solution.py:359
  16.9 0.8 %copy-start.1 = (f32[1,30,256]{2,0,1:T(1,128)S(1)}, f32[1,30,256]{2,0,1:T(1,128)}, u32[]{:S(2)}) copy-start(f32[1,30,256]{2,0,1:T(1,128)} %param.7) | copy-start | bytes 92164

commit v2 on v1

--- a/solution.py
+++ b/solution.py
@@ -297,6 +297,9 @@
         (mean_of(ref[...]), jnp.logical_and(other >= 0, other < times))
         for ref, other in ((near_ref, time + step), (far_ref, time - step))
     ]
+    drift_copy = pltpu.make_async_copy(drift_ref, drift_out, sem.at[0])
+    moved_copy = pltpu.make_async_copy(moved_ref, moved_out, sem.at[1])
+    moves = []
     for k in range(per_share):
         lanes = slice(k * LANES, (k + 1) * LANES)
         x = block_ref[pl.ds(first + k, features, stride=block_ref.shape[0] // features), :]
@@ -305,19 +308,16 @@
             gradient = gradient + jnp.where(present, (x - mean[:features, lanes]) / BRIDGE_VAR, 0.0)
         drift = -gradient
         drift_ref[:, 0, lanes] = drift
+        moves.append(x + LANGEVIN_STRIDE * drift)
+    drift_copy.start()
+    for k, move in enumerate(moves):
+        lanes = slice(k * LANES, (k + 1) * LANES)
         moved_ref[:, 0, lanes] = (
-            x
-            + LANGEVIN_STRIDE * drift
-            + math.sqrt(2.0 * LANGEVIN_STRIDE * NOISE_LEVEL) * noise_ref[:, 0, lanes]
+            move + math.sqrt(2.0 * LANGEVIN_STRIDE * NOISE_LEVEL) * noise_ref[:, 0, lanes]
         )
-    copies = [
-        pltpu.make_async_copy(drift_ref, drift_out, sem.at[0]),
-        pltpu.make_async_copy(moved_ref, moved_out, sem.at[1]),
-    ]
-    for copy in copies:
-        copy.start()
-    for copy in copies:
-        copy.wait()
+    moved_copy.start()
+    drift_copy.wait()
+    moved_copy.wait()
 
 
 VMEM = pl.BlockSpec(memory_space=pltpu.VMEM)

time: 18.6 us -> 18.6 us (level)
  no operation moved by 1% of the time
where the time goes in v2:
time: 18.6 us; the launch traced here: 18.4 us
  starting transfers between devices  7.95 us (43%)
  Pallas kernels  4.65 us (25%)
  waiting for transfers between devices  4.18 us (22%)
  local copies, waits for them, and re-layouts  0.93 us (5%)
  between operations  0.69 us (4%)
    ppermute x4, starting transfers between devices, over_time(): return lax.ppermute(block, ('tm', 'particle', 'cell'), pairs)  5.26 us
    pallas_call x6, Pallas kernels, call(): pl.pallas_call(kernel, out_shape=out_shape, in_specs=[VMEM] * len(args),...  4.65 us
    ppermute x2, waiting for transfers between devices, over_cell(): return lax.ppermute(x, 'cell', [(c, c ^ by) for c in range(cell_size)])  4.17 us
    ppermute x2, starting transfers between devices, over_cell(): return lax.ppermute(x, 'cell', [(c, c ^ by) for c in range(cell_size)])  2.69 us
    unnamed x8, local copies, waits for them, and re-layouts  0.93 us
  transfers between devices with their start and end apart: 6, of which 2 were waited for; matrix products, arithmetic and copies ran while one was open for 0% of the time, Pallas kernels for 21%

profile of v2, /device:TPU:0, one launch (start us, length us, event | category | flops | bytes accessed | tf_op | source)
XLA Modules:
  0.0 18.4 jit_solution(6316791075197760128)
XLA Ops:
  0.6 0.6 %collective-permute-start.1 = (f32[240,128]{1,0:T(8,128)}, f32[240,128]{1,0:T(8,128)S(1)}, u32[]{:S(2)}, u32[]{:S(2)}) collective-permute-start(f32[240,128]{1,0:T(8,128)} %bitcast.5), channel_id=1, source_target_pairs={{0,8},{1,9},{2,10},{3,11},{4,12},{5,13},{6,14},{7,15},{8,0},{9,1},... | collective-permute-start | bytes 368648 | tf_op jit(solution)/shard_map/ppermute | solution.py:368
  1.2 2.6 %collective-permute-start.2 = (f32[240,128]{1,0:T(8,128)}, f32[240,128]{1,0:T(8,128)S(1)}, u32[]{:S(2)}, u32[]{:S(2)}) collective-permute-start(f32[240,128]{1,0:T(8,128)} %bitcast.6), channel_id=1, source_target_pairs={{0,12},{1,13},{2,14},{3,15},{4,8},{5,9},{6,10},{7,11},{8,4},{9,5},... | collective-permute-start | bytes 368648 | tf_op jit(solution)/shard_map/ppermute | solution.py:368
  3.8 1.6 %collective-permute-start.3 = (f32[240,128]{1,0:T(8,128)}, f32[240,128]{1,0:T(8,128)S(1)}, u32[]{:S(2)}, u32[]{:S(2)}) collective-permute-start(f32[240,128]{1,0:T(8,128)} %bitcast.7), channel_id=1, source_target_pairs={{0,1},{1,0},{2,3},{3,2},{4,5},{5,4},{6,7},{7,6},{8,16},{9,17},{10,... | collective-permute-start | bytes 368648 | tf_op jit(solution)/shard_map/ppermute | solution.py:368
  5.4 0.5 %collective-permute-start.4 = (f32[240,128]{1,0:T(8,128)}, f32[240,128]{1,0:T(8,128)S(1)}, u32[]{:S(2)}, u32[]{:S(2)}) collective-permute-start(f32[240,128]{1,0:T(8,128)} %bitcast.8), channel_id=1, source_target_pairs={{0,4},{1,5},{2,6},{3,7},{4,0},{5,1},{6,2},{7,3},{8,20},{9,21},{10,... | collective-permute-start | bytes 368648 | tf_op jit(solution)/shard_map/ppermute | solution.py:368
  5.9 0.0 copy-start
  5.9 0.0 copy-start.2
  5.9 0.0 copy-start.3
  5.9 0.0 collective-permute-start
  5.9 0.9 %copy-done = f32[1,30,1024]{2,0,1:T(1,128)S(1)} copy-done((f32[1,30,1024]{2,0,1:T(1,128)S(1)}, f32[1,30,1024]{2,0,1:T(1,128)}, u32[]{:S(2)}) %copy-start) | copy-done | bytes 122904
  6.8 0.0 copy-done.2
  6.8 0.0 copy-done.3
  6.9 1.3 %shard_map.60 = (f32[2,32,256]{2,1,0:T(8,128)S(1)}, bf16[512,192]{1,0:T(8,128)(2,1)S(1)}, bf16[192,1024]{1,0:T(8,128)(2,1)S(1)}, s32[8,128]{1,0:T(8,128)S(1)}) custom-call(s32[4]{0:T(128)S(1)} %copy-done.3, s32[8,1024]{1,0:T(8,128)S(1)} %shard_map.59.positions_ref, f32[240,128]{1,0:T(8,128)S(1)} %bitcast.9, f32[240,128]{1,0:T(8,128)S(1)} %bitcast.14), custom_call_target="tpu_custom_call" | custom-call | flops 1000000000 | bytes 278544 | tf_op jit(solution)/shard_map/pallas_call | solution.py:327
  8.1 3.4 %collective-permute-done.refs_0_ = f32[240,128]{1,0:T(8,128)S(1)} collective-permute-done((f32[240,128]{1,0:T(8,128)}, f32[240,128]{1,0:T(8,128)S(1)}, u32[]{:S(2)}, u32[]{:S(2)}) %collective-permute-start) | collective-permute-done | bytes 122912 | tf_op jit(solution)/shard_map/ppermute | solution.py:359
  11.5 0.9 %shard_map.61 = (bf16[192,1024]{1,0:T(8,128)(2,1)S(1)}, f32[32,256]{1,0:T(8,128)S(1)}, f32[32,256]{1,0:T(8,128)S(1)}) custom-call(s32[8,128]{1,0:T(8,128)S(1)} %get-tuple-element.14.count_ref, s32[8,1024]{1,0:T(8,128)S(1)} %shard_map.59.positions_ref, bf16[512,192]{1,0:T(8,128)(2,1)S(1)} %get-tuple-element.15.queries_ref.fit_queries_ref, ...), custom_call_target="tpu_custom_call" | custom-call | flops 1000000000 | bytes 618496 | tf_op jit(solution)/shard_map/pallas_call | solution.py:327
  12.5 2.7 %collective-permute-start.5 = (f32[32,256]{1,0:T(8,128)S(1)}, f32[32,256]{1,0:T(8,128)S(1)}, u32[]{:S(2)}, u32[]{:S(2)}) collective-permute-start(f32[32,256]{1,0:T(8,128)S(1)} %get-tuple-element.23), channel_id=1, source_target_pairs={{0,2},{1,3},{2,0},{3,1},{4,6},{5,7},{6,4},{7,5},{8,10},{9,11},{10,... | collective-permute-start | bytes 98312 | tf_op jit(solution)/shard_map/ppermute | solution.py:359
  15.1 0.0 collective-permute-done.1.refs_2_
  15.1 0.0 collective-permute-done.2.refs_3_
  15.1 1.7 %shard_map.62 = (f32[32,256]{1,0:T(8,128)S(1)}, f32[32,256]{1,0:T(8,128)S(1)}, bf16[256,192]{1,0:T(8,128)(2,1)S(1)}) custom-call(f32[240,128]{1,0:T(8,128)S(1)} %bitcast.10, f32[32,256]{1,0:T(8,128)S(1)} %get-tuple-element.17.early_ref, bf16[512,192]{1,0:T(8,128)(2,1)S(1)} %get-tuple-element.15.queries_ref.fit_queries_ref, ...), custom_call_target="tpu_custom_call" | custom-call | flops 1000000000 | bytes 2367488 | tf_op jit(solution)/shard_map/pallas_call | solution.py:327
  16.8 0.0 collective-permute-done.3.refs_0_
  16.8 0.0 collective-permute-done.4.refs_1_
  16.9 0.0 copy-start.1
  16.9 0.8 %collective-permute-done.5.refs_1_ = f32[32,256]{1,0:T(8,128)S(1)} collective-permute-done((f32[32,256]{1,0:T(8,128)S(1)}, f32[32,256]{1,0:T(8,128)S(1)}, u32[]{:S(2)}, u32[]{:S(2)}) %collective-permute-start.5) | collective-permute-done | bytes 32800 | tf_op jit(solution)/shard_map/ppermute | solution.py:359
  17.7 0.0 copy-done.1
  17.7 0.7 %shard_map.64 = (f32[30,1,256]{2,1,0:T(1,128)}, f32[30,1,256]{2,1,0:T(1,128)}) custom-call(f32[240,128]{1,0:T(8,128)S(1)} %bitcast.11, f32[30,1,256]{2,1,0:T(1,128)S(1)} %bitcast.12, f32[32,256]{1,0:T(8,128)S(1)} %get-tuple-element.20.near_ref, f32[32,256]{1,0:T(8,128)S(1)} %shard_map.63.far_ref, f32[32,256]{1,0:T(8,128)S(1)} %get-tuple-element.22.refs_0_, ...), custom_call_target="tpu_custom_call" | custom-call | flops 1000000 | bytes 284672 | tf_op jit(solution)/shard_map/pallas_call | solution.py:327
  (2 shorter events, 0.0 us)
Async XLA Ops:
  0.6 14.5 %collective-permute-start.1 = (f32[240,128]{1,0:T(8,128)}, f32[240,128]{1,0:T(8,128)S(1)}, u32[]{:S(2)}, u32[]{:S(2)}) collective-permute-start(f32[240,128]{1,0:T(8,128)} %bitcast.5), channel_id=1, source_target_pairs={{0,8},{1,9},{2,10},{3,11},{4,12},{5,13},{6,14},{7,15},{8,0},{9,1},... | collective-permute-start | bytes 368648 | tf_op jit(solution)/shard_map/ppermute | solution.py:368
  1.2 14.0 %collective-permute-start.2 = (f32[240,128]{1,0:T(8,128)}, f32[240,128]{1,0:T(8,128)S(1)}, u32[]{:S(2)}, u32[]{:S(2)}) collective-permute-start(f32[240,128]{1,0:T(8,128)} %bitcast.6), channel_id=1, source_target_pairs={{0,12},{1,13},{2,14},{3,15},{4,8},{5,9},{6,10},{7,11},{8,4},{9,5},... | collective-permute-start | bytes 368648 | tf_op jit(solution)/shard_map/ppermute | solution.py:368
  3.8 13.0 %collective-permute-start.3 = (f32[240,128]{1,0:T(8,128)}, f32[240,128]{1,0:T(8,128)S(1)}, u32[]{:S(2)}, u32[]{:S(2)}) collective-permute-start(f32[240,128]{1,0:T(8,128)} %bitcast.7), channel_id=1, source_target_pairs={{0,1},{1,0},{2,3},{3,2},{4,5},{5,4},{6,7},{7,6},{8,16},{9,17},{10,... | collective-permute-start | bytes 368648 | tf_op jit(solution)/shard_map/ppermute | solution.py:368
  5.4 11.5 %collective-permute-start.4 = (f32[240,128]{1,0:T(8,128)}, f32[240,128]{1,0:T(8,128)S(1)}, u32[]{:S(2)}, u32[]{:S(2)}) collective-permute-start(f32[240,128]{1,0:T(8,128)} %bitcast.8), channel_id=1, source_target_pairs={{0,4},{1,5},{2,6},{3,7},{4,0},{5,1},{6,2},{7,3},{8,20},{9,21},{10,... | collective-permute-start | bytes 368648 | tf_op jit(solution)/shard_map/ppermute | solution.py:368
  5.9 0.9 %copy-start = (f32[1,30,1024]{2,0,1:T(1,128)S(1)}, f32[1,30,1024]{2,0,1:T(1,128)}, u32[]{:S(2)}) copy-start(f32[1,30,1024]{2,0,1:T(1,128)} %param.4) | copy-start | bytes 368644
  5.9 1.0 %copy-start.2 = (f32[1,30,1024]{2,0,1:T(1,128)S(1)}, f32[1,30,1024]{2,0,1:T(1,128)}, u32[]{:S(2)}) copy-start(f32[1,30,1024]{2,0,1:T(1,128)} %param.5) | copy-start | bytes 368644
  5.9 1.0 %copy-start.3 = (s32[4]{0:T(128)S(1)}, s32[4]{0:T(128)}, u32[]{:S(2)}) copy-start(s32[4]{0:T(128)} %counts_ref.1) | copy-start | bytes 52
  5.9 5.6 %collective-permute-start = (f32[240,128]{1,0:T(8,128)}, f32[240,128]{1,0:T(8,128)S(1)}, u32[]{:S(2)}, u32[]{:S(2)}) collective-permute-start(f32[240,128]{1,0:T(8,128)} %bitcast.13), channel_id=1, source_target_pairs={{0,1},{1,0},{2,3},{3,2},{4,5},{5,4},{6,7},{7,6},{8,9},{9,8},{10,11... | collective-permute-start | bytes 368648 | tf_op jit(solution)/shard_map/ppermute | solution.py:359
  12.5 5.2 %collective-permute-start.5 = (f32[32,256]{1,0:T(8,128)S(1)}, f32[32,256]{1,0:T(8,128)S(1)}, u32[]{:S(2)}, u32[]{:S(2)}) collective-permute-start(f32[32,256]{1,0:T(8,128)S(1)} %get-tuple-element.23), channel_id=1, source_target_pairs={{0,2},{1,3},{2,0},{3,1},{4,6},{5,7},{6,4},{7,5},{8,10},{9,11},{10,... | collective-permute-start | bytes 98312 | tf_op jit(solution)/shard_map/ppermute | solution.py:359
  16.9 0.8 %copy-start.1 = (f32[1,30,256]{2,0,1:T(1,128)S(1)}, f32[1,30,256]{2,0,1:T(1,128)}, u32[]{:S(2)}) copy-start(f32[1,30,256]{2,0,1:T(1,128)} %param.7) | copy-start | bytes 92164
